TPU v7x, 32 devices: a whole 2x2x4 slice. The times are simulated.
32 devices in a mesh: pipe: 4 (over x, core), dp: 8 (over z, y).
Axes of the slice: x: 2, y: 2, z: 4, core: 2. Of those that a mesh axis runs over, the one named last changes fastest.
Arguments:
- section_input: bfloat16 [4, 2048, 2048], P('pipe', 'dp'), may hold values from -6 to 6
- top_grad: bfloat16 [2048, 2048], P('dp'), may hold values from -6 to 6
- w_in: bfloat16 [4, 2048, 3072], P('pipe', 'dp'), may hold values from -0.125 to 0.125
- w_out: bfloat16 [4, 1024, 2048], P('pipe', 'dp'), may hold values from -0.1875 to 0.1875
- segments: int32 [16, 128], P('dp'), may hold values from 0 to 3, never falling along the last dimension, each value on 1 to 64 neighbouring positions
Outputs:
- section_grads: bfloat16 [4, 2048, 2048], P('pipe', 'dp')
- w_in_grad: float32 [4, 2048, 3072], P('pipe', 'dp')
- w_out_grad: float32 [4, 1024, 2048], P('pipe', 'dp')
Inputs may be any that keep to these rules, and one draw needn't show every extreme that they name: `segments`: in every row the history numbers run 0 to 3 without falling, each history has 1 to 64 positions, and one has exactly 64.
All inputs are finite; a program needn't handle non-finite values.
Results may differ from a plain program's by a relative error of at most 0.03.
Values may be sent and summed in bfloat16 or wider, within the bound.
A program may use at most 128 MiB of HBM per device.

v0:
```python
import jax
import jax.numpy as jnp
from jax import lax
from jax.sharding import PartitionSpec as P

HEADS = 16
QK_DIM = 32
V_DIM = 64


EPSILON = 1e-05


def passed_along(shard, axis, by):
    devices = lax.axis_size(axis)
    pairs = [(i, i + by) for i in range(devices) if 0 <= i + by < devices]
    return lax.ppermute(shard, axis, pairs)


def norm_rows(values):
    center = values - jnp.mean(values, axis=-1, keepdims=True)
    return center * lax.rsqrt(jnp.mean(center * center, axis=-1, keepdims=True) + EPSILON)


def silu_slope(preact):
    squash = jax.nn.sigmoid(preact)
    return squash * (1.0 + preact * (1.0 - squash))


def contract_rows(left, right):
    return lax.dot_general(
        left, right, (((0,), (0,)), ((), ())), preferred_element_type=jnp.float32
    )


def forward_front(inputs, w_first):
    normed = norm_rows(inputs.astype(jnp.float32)).astype(jnp.bfloat16)
    preact = jnp.dot(normed, w_first, preferred_element_type=jnp.float32)
    return (normed, preact, jax.nn.silu(preact).astype(jnp.bfloat16))


def attend(activated, history):
    row_count = activated.shape[0]
    value_cols = HEADS * V_DIM
    query_cols = HEADS * QK_DIM
    active32 = activated.astype(jnp.float32)
    gating = active32[:, :value_cols]
    values = active32[:, value_cols : 2 * value_cols].reshape(row_count, HEADS, V_DIM)
    queries = active32[:, 2 * value_cols : 2 * value_cols + query_cols].reshape(
        row_count, HEADS, QK_DIM
    )
    key_rows = active32[:, 2 * value_cols + query_cols :].reshape(row_count, HEADS, QK_DIM)
    scores = jnp.einsum("qhd,khd->hqk", queries, key_rows) * QK_DIM ** (-0.5)
    same_doc = history[:, None] == history[None, :]
    positions = lax.broadcasted_iota(jnp.int32, (row_count, row_count), 0)
    columns = lax.broadcasted_iota(jnp.int32, (row_count, row_count), 1)
    allowed = jnp.logical_and(same_doc, columns <= positions)
    counts = jnp.sum(same_doc.astype(jnp.float32), axis=1)
    weights_mask = allowed.astype(jnp.float32) / counts[:, None]
    weights = jax.nn.silu(scores) * weights_mask[None]
    mixed = jnp.einsum("hqk,khd->qhd", weights, values).reshape(row_count, value_cols)
    return norm_rows(mixed) * gating


def layer_back(inputs, preact, activated, upstream, history, w_first, w_second):
    gated_full, pull = jax.vjp(lambda active_in: attend(active_in, history), activated)
    gated = gated_full.astype(jnp.bfloat16)
    grad_second = contract_rows(gated, upstream)
    grad_gated = lax.dot_general(
        upstream, w_second, (((1,), (1,)), ((), ())), preferred_element_type=jnp.float32
    )
    (grad_active,) = pull(grad_gated)
    grad_preact = (grad_active.astype(jnp.float32) * silu_slope(preact)).astype(jnp.bfloat16)
    grad_normed = lax.dot_general(
        grad_preact, w_first, (((1,), (1,)), ((), ())), preferred_element_type=jnp.float32
    )
    _, pull_norm = jax.vjp(norm_rows, inputs.astype(jnp.float32))
    (grad_through,) = pull_norm(grad_normed)
    grad_input = (upstream.astype(jnp.float32) + grad_through).astype(jnp.bfloat16)
    return (grad_input, grad_preact, grad_second)


def body(section_input, top_grad, w_in, w_out, segments):
    w_first = lax.all_gather(w_in[0], "dp", axis=0, tiled=True)
    w_second = lax.all_gather(w_out[0], "dp", axis=0, tiled=True)
    sections = lax.axis_size("pipe")
    section = lax.axis_index("pipe")
    inputs_all = section_input[0]
    micro = segments.shape[0]
    length = segments.shape[1]
    width = inputs_all.shape[1]
    hidden_cols = w_first.shape[1]
    store = jnp.zeros((micro * length, hidden_cols), jnp.bfloat16)

    def one_step(step_index, carry):
        incoming, store_now, acc_out, grads = carry
        slot = step_index - (sections - 1 - section)
        active = jnp.logical_and(slot >= 0, slot < micro)
        slot = jnp.clip(slot, 0, micro - 1)
        start = slot * length
        top_rows = lax.dynamic_slice_in_dim(top_grad, start, length, 0)
        upstream = jnp.where(section == sections - 1, top_rows, incoming)
        history = lax.dynamic_index_in_dim(segments, slot, 0, keepdims=False)

        def work():
            inputs = lax.dynamic_slice_in_dim(inputs_all, start, length, 0)
            normed, preact, activated = forward_front(inputs, w_first)
            grad_input, grad_preact, grad_second = layer_back(
                inputs, preact, activated, upstream, history, w_first, w_second
            )
            store_next = lax.dynamic_update_slice_in_dim(store_now, grad_preact, start, 0)
            grads_next = lax.dynamic_update_slice_in_dim(grads, grad_input, start, 0)
            return (grad_input, store_next, acc_out + grad_second, grads_next)

        def resting():
            return (jnp.zeros_like(incoming), store_now, acc_out, grads)

        outgoing, store_now, acc_out, grads = lax.cond(active, work, resting)
        incoming = passed_along(outgoing, "pipe", -1)
        return (incoming, store_now, acc_out, grads)

    start_carry = (
        jnp.zeros((length, width), jnp.bfloat16),
        store,
        jnp.zeros((w_second.shape[0], width), jnp.float32),
        jnp.zeros_like(inputs_all),
    )
    _, store, acc_out, grads = lax.fori_loop(0, sections + micro - 1, one_step, start_carry)
    normed_rows = norm_rows(inputs_all.astype(jnp.float32)).astype(jnp.bfloat16)
    grad_first = lax.psum_scatter(
        contract_rows(normed_rows, store).astype(jnp.bfloat16),
        "dp",
        scatter_dimension=0,
        tiled=True,
    ).astype(jnp.float32)
    grad_out = lax.psum_scatter(
        acc_out.astype(jnp.bfloat16), "dp", scatter_dimension=0, tiled=True
    ).astype(jnp.float32)
    return (grads[None], grad_first[None], grad_out[None])


def solution(mesh):
    return jax.shard_map(
        body,
        mesh=mesh,
        in_specs=(
            P("pipe", "dp", None),
            P("dp", None),
            P("pipe", "dp", None),
            P("pipe", "dp", None),
            P("dp", None),
        ),
        out_specs=(P("pipe", "dp", None), P("pipe", "dp", None), P("pipe", "dp", None)),
        check_vma=False,
    )
```

profile of v0, /device:TPU:0, one launch (start us, length us, event | category | flops | bytes accessed | tf_op | source)
XLA Modules:
  0.0 868.3 jit_solution(9166335217495823203)
XLA Ops:
  8.7 76.9 %all-gather.5.cloned.1.call-done = bf16[1,1024,2048]{2,1,0:T(8,128)(2,1)} async-done(((bf16[1,128,2048]{2,1,0:T(8,128)(2,1)}), bf16[1,1024,2048]{2,1,0:T(8,128)(2,1)}) %all-gather.5.cloned.1.call-update) | async-done | bytes 4194320 | tf_op jit(solution)/shard_map/all_gather | solution.py:85
  85.6 176.9 %all-gather.7.cloned.1.call-done = bf16[1,2048,3072]{2,1,0:T(8,128)(2,1)} async-done(((bf16[1,256,3072]{2,1,0:T(8,128)(2,1)}), bf16[1,2048,3072]{2,1,0:T(8,128)(2,1)}) %all-gather.7.cloned.1.call-update) | async-done | bytes 12582928 | tf_op jit(solution)/shard_map/all_gather | solution.py:84
  264.7 4.3 broadcast_in_dim.57
  270.0 285.4 %while.21 = (s32[]{:T(128)}, bf16[128,2048]{1,0:T(8,128)(2,1)}, bf16[256,3072]{1,0:T(8,128)(2,1)}, f32[1024,2048]{1,0:T(8,128)}, bf16[256,2048]{1,0:T(8,128)(2,1...) while((s32[]{:T(128)}, bf16[128,2048]{1,0:T(8,128)(2,1)}, ...), condition=%wide.region_12.13_spmd, body=%wide.region_0.12_spmd.sunk | while | flops 4473488384 | bytes 157841232 | solution.py:128
  272.2 2.7 collective-permute-done
  277.8 8.8 %collective-permute-done = bf16[128,2048]{1,0:T(8,128)(2,1)S(1)} collective-permute-done((bf16[128,2048]{1,0:T(8,128)(2,1)}, bf16[128,2048]{1,0:T(8,128)(2,1)S(1)}, u32[]{:S(2)}, u32[]{:S(2)}) %collective-permute-start) | collective-permute-done | bytes 524320 | tf_op jit(solution)/shard_map/while/body/eval_jaxpr/ppermute | solution.py:17
  289.5 148.4 %collective-permute-done = bf16[128,2048]{1,0:T(8,128)(2,1)S(1)} collective-permute-done((bf16[128,2048]{1,0:T(8,128)(2,1)}, bf16[128,2048]{1,0:T(8,128)(2,1)S(1)}, u32[]{:S(2)}, u32[]{:S(2)}) %collective-permute-start) | collective-permute-done | bytes 524320 | tf_op jit(solution)/shard_map/while/body/eval_jaxpr/ppermute | solution.py:17
  438.8 50.1 %conditional.2 = (bf16[128,2048]{1,0:T(8,128)(2,1)}, bf16[256,3072]{1,0:T(8,128)(2,1)}, f32[1024,2048]{1,0:T(8,128)}, bf16[256,2048]{1,0:T(8,128)(2,1)}) conditional(s32[]{:T(128)} %convert_element_type.154, (bf16[256,3072]{1,0:T(8,128)(2,1)}, f32[1024,2048]{1,0:T(8,128)}, bf16[256,2048]{1,0:T(8,128)(2,1)}) %tuple.69, (pred[]{:T(512)}, s32[]{:T(128)}, ...), branch_computations={%region_1.1_spmd, %region_2.11_spmd} | conditional | flops 4473488384 | bytes 153646560 | solution.py:118
  439.3 7.9 multiply_convert_fusion.1
  451.2 3.8 multiply_reduce_fusion
  456.5 2.6 fusion.22
  460.4 2.1 fusion.9
  466.1 2.0 fusion.43
  469.9 3.2 constant_dynamic-update-slice_fusion
  473.1 9.0 %fusion.6 = (f32[128]{0:T(128)S(1)}, f32[128,2048]{1,0:T(8,128)S(1)}) fusion(f32[128]{0:T(128)S(1)} %broadcast_multiply_fusion.1, bf16[256,2048]{1,0:T(8,128)(2,1)S(1)} %get-tuple-element.374, s32[]{:T(128)S(6)} %select_n.43, bf16[128,3072]{1,0:T(8,128)(2,1)S(1)} %get-tuple-element.433, bf16[2048,3072]{1,0:T(8,128)(2,1)} %get-tuple-element.375), kind=kOutput, calls=%fused_computation.17 | convolution fusion | flops 1611661184 | bytes 14943236 | tf_op jit(solution)/shard_map/while/body/eval_jaxpr/cond/branch_1_fun/dot_general | solution.py:74
  485.7 3.2 copy-done
  490.2 9.4 %collective-permute-done = bf16[128,2048]{1,0:T(8,128)(2,1)S(1)} collective-permute-done((bf16[128,2048]{1,0:T(8,128)(2,1)}, bf16[128,2048]{1,0:T(8,128)(2,1)S(1)}, u32[]{:S(2)}, u32[]{:S(2)}) %collective-permute-start) | collective-permute-done | bytes 524320 | tf_op jit(solution)/shard_map/while/body/eval_jaxpr/ppermute | solution.py:17
  500.4 50.1 %conditional.2 = (bf16[128,2048]{1,0:T(8,128)(2,1)}, bf16[256,3072]{1,0:T(8,128)(2,1)}, f32[1024,2048]{1,0:T(8,128)}, bf16[256,2048]{1,0:T(8,128)(2,1)}) conditional(s32[]{:T(128)} %convert_element_type.154, (bf16[256,3072]{1,0:T(8,128)(2,1)}, f32[1024,2048]{1,0:T(8,128)}, bf16[256,2048]{1,0:T(8,128)(2,1)}) %tuple.69, (pred[]{:T(512)}, s32[]{:T(128)}, ...), branch_computations={%region_1.1_spmd, %region_2.11_spmd} | conditional | flops 4473488384 | bytes 153646560 | solution.py:118
  500.9 7.9 multiply_convert_fusion.1
  512.9 3.8 multiply_reduce_fusion
  518.2 2.6 fusion.22
  522.0 2.1 fusion.9
  531.5 3.2 constant_dynamic-update-slice_fusion
  534.8 9.0 %fusion.6 = (f32[128]{0:T(128)S(1)}, f32[128,2048]{1,0:T(8,128)S(1)}) fusion(f32[128]{0:T(128)S(1)} %broadcast_multiply_fusion.1, bf16[256,2048]{1,0:T(8,128)(2,1)S(1)} %get-tuple-element.374, s32[]{:T(128)S(6)} %select_n.43, bf16[128,3072]{1,0:T(8,128)(2,1)S(1)} %get-tuple-element.433, bf16[2048,3072]{1,0:T(8,128)(2,1)} %get-tuple-element.375), kind=kOutput, calls=%fused_computation.17 | convolution fusion | flops 1611661184 | bytes 14943236 | tf_op jit(solution)/shard_map/while/body/eval_jaxpr/cond/branch_1_fun/dot_general | solution.py:74
  547.4 3.2 copy-done
  551.9 2.7 collective-permute-done
  555.4 6.0 convert_element_type.89
  562.1 8.0 convolution_convert_fusion
  570.2 77.7 %reduce-scatter.5.cloned.1.call-done = bf16[128,2048]{1,0:T(8,128)(2,1)} async-done(((bf16[1024,2048]{1,0:T(8,128)(2,1)}), bf16[128,2048]{1,0:T(8,128)(2,1)}) %reduce-scatter.5.cloned.1.call-update) | async-done | bytes 524304 | tf_op jit(solution)/shard_map/reduce_scatter | solution.py:136
  647.9 2.1 bitcast_convert_fusion.1
  650.0 208.4 %reduce-scatter.3.cloned.1.call-done = bf16[256,3072]{1,0:T(8,128)(2,1)} async-done(((bf16[2048,3072]{1,0:T(8,128)(2,1)}), bf16[256,3072]{1,0:T(8,128)(2,1)}) %reduce-scatter.3.cloned.1.call-update) | async-done | bytes 1572880 | tf_op jit(solution)/shard_map/reduce_scatter | solution.py:130
  858.4 3.4 bitcast_convert_fusion
  (151 shorter events, 55.2 us)
Async XLA Ops:
  7.2 78.5 %all-gather.5.cloned.1.call-start = ((), (), s32[]{:S(2)}) async-start(), calls=%async_computation.4 | async-start | bytes 4718592 | tf_op jit(solution)/shard_map/all_gather | solution.py:85
  7.9 254.6 %all-gather.7.cloned.1.call-start = ((), (), s32[]{:S(2)}) async-start(), calls=%async_computation.5 | async-start | bytes 14155776 | tf_op jit(solution)/shard_map/all_gather | solution.py:84
  8.6 639.2 %reduce-scatter.5.cloned.1.call-start = ((), (), s32[]{:S(2)}) async-start(), calls=%async_computation.3 | async-start | bytes 4718592 | tf_op jit(solution)/shard_map/reduce_scatter | solution.py:136
  264.7 5.4 copy-start.1
  270.9 4.0 collective-permute-start
  276.5 10.1 %collective-permute-start = (bf16[128,2048]{1,0:T(8,128)(2,1)}, bf16[128,2048]{1,0:T(8,128)(2,1)S(1)}, u32[]{:S(2)}, u32[]{:S(2)}) collective-permute-start(bf16[128,2048]{1,0:T(8,128)(2,1)} %get-tuple-element.526), channel_id=1, source_target_pairs={{8,0},{16,8},{24,16},{9,1},{17,9},{25,17},{10,2},{18,10},{26,18},{... | collective-permute-start | bytes 1572872 | tf_op jit(solution)/shard_map/while/body/eval_jaxpr/ppermute | solution.py:17
  286.6 0.8 copy-start.6
  288.3 149.7 %collective-permute-start = (bf16[128,2048]{1,0:T(8,128)(2,1)}, bf16[128,2048]{1,0:T(8,128)(2,1)S(1)}, u32[]{:S(2)}, u32[]{:S(2)}) collective-permute-start(bf16[128,2048]{1,0:T(8,128)(2,1)} %get-tuple-element.526), channel_id=1, source_target_pairs={{8,0},{16,8},{24,16},{9,1},{17,9},{25,17},{10,2},{18,10},{26,18},{... | collective-permute-start | bytes 1572872 | tf_op jit(solution)/shard_map/while/body/eval_jaxpr/ppermute | solution.py:17
  439.2 7.9 copy-start.10
  447.3 2.2 copy-start.7
  447.6 1.9 copy-start.3
  448.0 1.6 copy-start.5
  456.5 2.6 copy-start.8
  460.3 2.9 copy-start.4
  469.9 14.1 %slice-start = ((s8[8388608]{0:T(1024)(128)(4,1)}), s8[4194304]{0:T(1024)(128)(4,1)S(1)}, s32[]{:S(2)}) async-start(s8[8388608]{0:T(1024)(128)(4,1)} %bitcast.58), calls=%async_computation.6 | async-start | bytes 8388608 | tf_op jit(solution)/shard_map/while/body/eval_jaxpr/cond
  473.1 9.0 %copy-start.11 = (f32[128]{0:T(128)S(1)}, f32[128]{0:T(128)}, u32[]{:S(2)}) copy-start(f32[128]{0:T(128)} %copy-done.10) | copy-start | bytes 1540 | tf_op jit(solution)/shard_map/while/body/eval_jaxpr/cond
  473.1 10.9 %slice-start.1 = ((s8[8388608]{0:T(1024)(128)(4,1)}), s8[4194304]{0:T(1024)(128)(4,1)S(1)}, s32[]{:S(2)}) async-start(s8[8388608]{0:T(1024)(128)(4,1)} %bitcast.58), calls=%async_computation.7 | async-start | bytes 8388608 | tf_op jit(solution)/shard_map/while/body/eval_jaxpr/cond
  485.7 3.2 copy-start
  488.9 10.7 %collective-permute-start = (bf16[128,2048]{1,0:T(8,128)(2,1)}, bf16[128,2048]{1,0:T(8,128)(2,1)S(1)}, u32[]{:S(2)}, u32[]{:S(2)}) collective-permute-start(bf16[128,2048]{1,0:T(8,128)(2,1)} %get-tuple-element.526), channel_id=1, source_target_pairs={{8,0},{16,8},{24,16},{9,1},{17,9},{25,17},{10,2},{18,10},{26,18},{... | collective-permute-start | bytes 1572872 | tf_op jit(solution)/shard_map/while/body/eval_jaxpr/ppermute | solution.py:17
  499.6 0.8 copy-start.6
  500.9 7.9 copy-start.10
  509.0 2.2 copy-start.7
  509.3 1.9 copy-start.3
  509.6 1.6 copy-start.5
  518.1 2.6 copy-start.8
  522.0 2.9 copy-start.4
  531.5 14.1 %slice-start = ((s8[8388608]{0:T(1024)(128)(4,1)}), s8[4194304]{0:T(1024)(128)(4,1)S(1)}, s32[]{:S(2)}) async-start(s8[8388608]{0:T(1024)(128)(4,1)} %bitcast.58), calls=%async_computation.6 | async-start | bytes 8388608 | tf_op jit(solution)/shard_map/while/body/eval_jaxpr/cond
  534.8 9.0 %copy-start.11 = (f32[128]{0:T(128)S(1)}, f32[128]{0:T(128)}, u32[]{:S(2)}) copy-start(f32[128]{0:T(128)} %copy-done.10) | copy-start | bytes 1540 | tf_op jit(solution)/shard_map/while/body/eval_jaxpr/cond
  534.8 10.9 %slice-start.1 = ((s8[8388608]{0:T(1024)(128)(4,1)}), s8[4194304]{0:T(1024)(128)(4,1)S(1)}, s32[]{:S(2)}) async-start(s8[8388608]{0:T(1024)(128)(4,1)} %bitcast.58), calls=%async_computation.7 | async-start | bytes 8388608 | tf_op jit(solution)/shard_map/while/body/eval_jaxpr/cond
  547.4 3.2 copy-start
  550.6 4.0 collective-permute-start
  561.4 296.9 %reduce-scatter.3.cloned.1.call-start = ((), (), s32[]{:S(2)}) async-start(), calls=%async_computation.2 | async-start | bytes 14155776 | tf_op jit(solution)/shard_map/reduce_scatter | solution.py:130
  (7 other events, 5.3 us)
Sparse Core Ops, SparseCore 0:
  10.1 75.5 all-gather.4
  87.8 174.6 all-gather.6
  561.5 86.2 reduce-scatter.4
  651.3 207.0 reduce-scatter.2
where the time goes:
time: 869 us; the launch traced here: 868 us
  waiting for transfers between devices  713 us (82%)
  matrix products  70 us (8%)
  local copies, waits for them, and re-layouts  35.1 us (4%)
  other arithmetic  29.1 us (3%)
  between operations  13.8 us (2%)
    reduce_scatter x1, waiting for transfers between devices, body(): lax.psum_scatter(contract_rows(normed_rows, store).astype(jnp.bfloat16),...  208 us
    all_gather x1, waiting for transfers between devices, body(): w_first = lax.all_gather(w_in[0], 'dp', axis=0, tiled=True)  177 us
    ppermute x5, waiting for transfers between devices, passed_along(): return lax.ppermute(shard, axis, pairs)  172 us
    reduce_scatter x1, waiting for transfers between devices, body(): lax.psum_scatter(acc_out.astype(jnp.bfloat16), 'dp', scatter_dimension=0,...  77.7 us
    all_gather x1, waiting for transfers between devices, body(): w_second = lax.all_gather(w_out[0], 'dp', axis=0, tiled=True)  76.9 us
    dot_general x2, matrix products, layer_back(): lax.dot_general(grad_preact, w_first, (((1,), (1,)), ((), ())), preferred...  18.1 us
  transfers between devices with their start and end apart: 9, of which 9 were waited for; matrix products, arithmetic and copies ran while one was open for 1% of the time, Pallas kernels for 0%

commit v1 on v0

v1 whole, which is shorter than its diff:
```python
import functools

import jax
import jax.numpy as jnp
from jax import lax
from jax.experimental import pallas as pl
from jax.experimental.pallas import tpu as pltpu
from jax.sharding import PartitionSpec as P

HEADS = 16
QK_DIM = 32
V_DIM = 64
LANES = 128

EPSILON = 1e-05
MESH = pl.DeviceIdType.MESH
VMEM = pl.BlockSpec(memory_space=pltpu.VMEM)

QK_HEADS = LANES // QK_DIM
V_HEADS = LANES // V_DIM
GROUPS = HEADS // QK_HEADS
V_COLS = HEADS * V_DIM
Q_COLS = HEADS * QK_DIM
GROUP_V = QK_HEADS * V_DIM
SCALE = QK_DIM ** (-0.5)


def norm_rows(values):
    center = values - jnp.mean(values, axis=-1, keepdims=True)
    return center * lax.rsqrt(jnp.mean(center * center, axis=-1, keepdims=True) + EPSILON)


def silu_slope(preact):
    squash = jax.nn.sigmoid(preact)
    return squash * (1.0 + preact * (1.0 - squash))


def dot_nt(left, right):
    return lax.dot_general(
        left, right, (((1,), (1,)), ((), ())), preferred_element_type=jnp.float32
    )


def dot_nn(left, right):
    return lax.dot_general(
        left, right, (((1,), (0,)), ((), ())), preferred_element_type=jnp.float32
    )


def contract_rows(left, right):
    return lax.dot_general(
        left, right, (((0,), (0,)), ((), ())), preferred_element_type=jnp.float32
    )


def only_head(block, lane, width, index):
    keep = jnp.logical_and(lane >= index * width, lane < (index + 1) * width)
    return jnp.where(keep, block, jnp.zeros_like(block))


def at(start, size):
    return pl.ds(pl.multiple_of(start, LANES), size)


def attend_kernel(micro, length, act_ref, mask_ref, score_ref, unit_ref, rstd_ref, gated_ref, mixed):
    lane = lax.broadcasted_iota(jnp.int32, (length, LANES), 1)

    def one(index, _):
        slot, group = index // GROUPS, index % GROUPS
        rows = at(slot * length, length)
        queries = act_ref[rows, at(2 * V_COLS + group * LANES, LANES)]
        keys = act_ref[rows, at(2 * V_COLS + Q_COLS + group * LANES, LANES)]
        mask = mask_ref[rows, :]
        for half in range(GROUP_V // LANES):
            cols = group * GROUP_V + half * LANES
            values = act_ref[rows, at(V_COLS + cols, LANES)]
            total = jnp.zeros((length, LANES), jnp.float32)
            for sub in range(V_HEADS):
                head = half * V_HEADS + sub
                score = dot_nt(only_head(queries, lane, QK_DIM, head), keys) * SCALE
                score_ref[at((index * QK_HEADS + head) * length, length), :] = score
                weight = (jax.nn.silu(score) * mask).astype(jnp.bfloat16)
                total += dot_nn(weight, only_head(values, lane, V_DIM, sub))
            mixed[rows, at(cols, LANES)] = total
        return 0

    lax.fori_loop(0, micro * GROUPS, one, 0)

    def finish(slot, _):
        rows = at(slot * length, length)
        value = mixed[rows, :]
        center = value - jnp.mean(value, axis=-1, keepdims=True)
        rstd = lax.rsqrt(jnp.mean(center * center, axis=-1, keepdims=True) + EPSILON)
        unit = center * rstd
        unit_ref[rows, :] = unit
        rstd_ref[rows, :] = jnp.broadcast_to(rstd, (length, LANES))
        gated_ref[rows, :] = (unit * act_ref[rows, :V_COLS].astype(jnp.float32)).astype(jnp.bfloat16)
        return 0

    lax.fori_loop(0, micro, finish, 0)


def attend(activated, mask, micro, length):
    tokens = micro * length
    return pl.pallas_call(
        functools.partial(attend_kernel, micro, length),
        out_shape=(
            jax.ShapeDtypeStruct((micro * HEADS * length, length), jnp.float32),
            jax.ShapeDtypeStruct((tokens, V_COLS), jnp.float32),
            jax.ShapeDtypeStruct((tokens, LANES), jnp.float32),
            jax.ShapeDtypeStruct((tokens, V_COLS), jnp.bfloat16),
        ),
        in_specs=[VMEM] * 2,
        out_specs=(VMEM,) * 4,
        scratch_shapes=[pltpu.VMEM((tokens, V_COLS), jnp.float32)],
        name="attend",
    )(activated, mask)


def chain_kernel(
    micro, length, sections,
    top_ref, input_ref, act_ref, pre_ref, score_ref, unit_ref, rstd_ref, mask_ref, first_ref, second_ref,
    up_ref, gpre_ref, gin_ref,
    landed, leaving, ggate, dmix, gnorm, send_sem, recv_sem,
):
    section = lax.axis_index("pipe")
    width = input_ref.shape[1]
    tile = 2 * LANES
    lane = lax.broadcasted_iota(jnp.int32, (length, LANES), 1)
    is_last = section == sections - 1
    is_first = section == 0

    barrier = pltpu.get_barrier_semaphore()

    @pl.when(jnp.logical_not(is_last))
    def _():
        pl.semaphore_signal(
            barrier, inc=1, device_id={"pipe": jnp.minimum(section + 1, sections - 1)}, device_id_type=MESH
        )

    @pl.when(jnp.logical_not(is_first))
    def _():
        pl.semaphore_wait(barrier, 1)

    def copy_of(slot):
        return pltpu.make_async_remote_copy(
            src_ref=leaving.at[slot],
            dst_ref=landed.at[slot],
            send_sem=send_sem.at[slot],
            recv_sem=recv_sem.at[slot],
            device_id={"pipe": jnp.maximum(section - 1, 0)},
            device_id_type=MESH,
        )

    def store_grad(rows, cols, size, value):
        rounded = value.astype(jnp.bfloat16).astype(jnp.float32)
        gpre_ref[rows, at(cols, size)] = (
            rounded * silu_slope(pre_ref[rows, at(cols, size)])
        ).astype(jnp.bfloat16)

    for slot in range(micro):
        rows = pl.ds(slot * length, length)

        @pl.when(is_last)
        def _():
            up_ref[rows, :] = top_ref[rows, :]

        @pl.when(jnp.logical_not(is_last))
        def _():
            copy_of(slot).wait_recv()
            up_ref[rows, :] = landed[slot]

        def gate_tile(index, _):
            ggate[:, at(index * tile, tile)] = dot_nt(up_ref[rows, :], second_ref[at(index * tile, tile), :])
            return 0

        lax.fori_loop(0, V_COLS // tile, gate_tile, 0)
        gating = act_ref[rows, :V_COLS].astype(jnp.float32)
        unit = unit_ref[rows, :]
        grad = ggate[...]
        store_grad(rows, 0, V_COLS, grad * unit)
        grad = grad * gating
        mean_grad = jnp.mean(grad, axis=-1, keepdims=True)
        mean_unit = jnp.mean(grad * unit, axis=-1, keepdims=True)
        dmix[...] = (rstd_ref[rows, :1] * (grad - mean_grad - unit * mean_unit)).astype(jnp.bfloat16)

        def one(group, _):
            queries = act_ref[rows, at(2 * V_COLS + group * LANES, LANES)]
            keys = act_ref[rows, at(2 * V_COLS + Q_COLS + group * LANES, LANES)]
            mask = mask_ref[rows, :]
            grad_q = jnp.zeros((length, LANES), jnp.float32)
            grad_k = jnp.zeros((length, LANES), jnp.float32)
            for half in range(GROUP_V // LANES):
                cols = group * GROUP_V + half * LANES
                values = act_ref[rows, at(V_COLS + cols, LANES)]
                grad_mix = dmix[:, at(cols, LANES)]
                grad_v = jnp.zeros((length, LANES), jnp.float32)
                for sub in range(V_HEADS):
                    head = half * V_HEADS + sub
                    mix_head = only_head(grad_mix, lane, V_DIM, sub)
                    place = (slot * HEADS + group * QK_HEADS + head) * length
                    score = score_ref[at(place, length), :]
                    squash = jax.nn.sigmoid(score)
                    weight = (score * squash * mask).astype(jnp.bfloat16)
                    slope = squash * (1.0 + score * (1.0 - squash)) * mask * SCALE
                    grad_score = (dot_nt(mix_head, values) * slope).astype(jnp.bfloat16)
                    grad_v += contract_rows(weight, mix_head)
                    grad_q += dot_nn(grad_score, only_head(keys, lane, QK_DIM, head))
                    grad_k += contract_rows(grad_score, only_head(queries, lane, QK_DIM, head))
                store_grad(rows, V_COLS + cols, LANES, grad_v)
            store_grad(rows, 2 * V_COLS + group * LANES, LANES, grad_q)
            store_grad(rows, 2 * V_COLS + Q_COLS + group * LANES, LANES, grad_k)
            return 0

        lax.fori_loop(0, GROUPS, one, 0)

        def norm_tile(index, _):
            gnorm[:, at(index * tile, tile)] = dot_nt(gpre_ref[rows, :], first_ref[at(index * tile, tile), :])
            return 0

        lax.fori_loop(0, width // tile, norm_tile, 0)
        value = input_ref[rows, :].astype(jnp.float32)
        center = value - jnp.mean(value, axis=-1, keepdims=True)
        rstd = lax.rsqrt(jnp.mean(center * center, axis=-1, keepdims=True) + EPSILON)
        unit = center * rstd
        grad = gnorm[...]
        mean_grad = jnp.mean(grad, axis=-1, keepdims=True)
        mean_unit = jnp.mean(grad * unit, axis=-1, keepdims=True)
        through = rstd * (grad - mean_grad - unit * mean_unit)
        result = (up_ref[rows, :].astype(jnp.float32) + through).astype(jnp.bfloat16)
        leaving[slot] = result
        gin_ref[rows, :] = result

        @pl.when(jnp.logical_not(is_first))
        def _():
            copy_of(slot).start()

    for slot in range(micro):

        @pl.when(jnp.logical_not(is_first))
        def _():
            copy_of(slot).wait_send()


def chain(top, inputs, activated, preact, scores, unit, rstd, mask, w_first, w_second, micro, length):
    tokens, width = inputs.shape
    return pl.pallas_call(
        functools.partial(chain_kernel, micro, length, lax.axis_size("pipe")),
        out_shape=(
            jax.ShapeDtypeStruct((tokens, width), jnp.bfloat16),
            jax.ShapeDtypeStruct(preact.shape, jnp.bfloat16),
            jax.ShapeDtypeStruct((tokens, width), jnp.bfloat16),
        ),
        in_specs=[VMEM] * 10,
        out_specs=(VMEM,) * 3,
        scratch_shapes=[
            pltpu.VMEM((micro, length, width), jnp.bfloat16),
            pltpu.VMEM((micro, length, width), jnp.bfloat16),
            pltpu.VMEM((length, V_COLS), jnp.float32),
            pltpu.VMEM((length, V_COLS), jnp.bfloat16),
            pltpu.VMEM((length, width), jnp.float32),
            pltpu.SemaphoreType.DMA((micro,)),
            pltpu.SemaphoreType.DMA((micro,)),
        ],
        compiler_params=pltpu.CompilerParams(
            collective_id=0, has_side_effects=True, vmem_limit_bytes=60 * 1024 * 1024
        ),
        name="chain",
    )(top, inputs, activated, preact, scores, unit, rstd, mask, w_first, w_second)


def mask_of(segments):
    length = segments.shape[1]
    same = segments[:, :, None] == segments[:, None, :]
    positions = lax.broadcasted_iota(jnp.int32, (length, length), 0)
    columns = lax.broadcasted_iota(jnp.int32, (length, length), 1)
    counts = jnp.sum(same.astype(jnp.float32), axis=2, keepdims=True)
    allowed = jnp.logical_and(same, (columns <= positions)[None])
    return (allowed.astype(jnp.float32) / counts).reshape(-1, length)


def body(section_input, top_grad, w_in, w_out, segments):
    micro, length = segments.shape
    inputs = section_input[0]
    w_first = lax.all_gather(w_in[0], "dp", axis=0, tiled=True)
    w_mine, w_first = lax.optimization_barrier((w_out[0], w_first))
    w_second = lax.all_gather(w_mine, "dp", axis=0, tiled=True)
    mask = mask_of(segments)
    normed = norm_rows(inputs.astype(jnp.float32)).astype(jnp.bfloat16)
    preact = jnp.dot(normed, w_first, preferred_element_type=jnp.float32)
    activated = jax.nn.silu(preact).astype(jnp.bfloat16)
    scores, unit, rstd, gated = attend(activated, mask, micro, length)
    upstream, grad_preact, grads = chain(
        top_grad, inputs, activated, preact, scores, unit, rstd, mask, w_first, w_second, micro, length
    )
    part_out = contract_rows(gated, upstream).astype(jnp.bfloat16)
    grad_out = lax.psum_scatter(part_out, "dp", scatter_dimension=0, tiled=True).astype(jnp.float32)
    part_in = contract_rows(normed, grad_preact).astype(jnp.bfloat16)
    grad_first = lax.psum_scatter(part_in, "dp", scatter_dimension=0, tiled=True).astype(jnp.float32)
    return (grads[None], grad_first[None], grad_out[None])


def solution(mesh):
    return jax.shard_map(
        body,
        mesh=mesh,
        in_specs=(
            P("pipe", "dp", None),
            P("dp", None),
            P("pipe", "dp", None),
            P("pipe", "dp", None),
            P("dp", None),
        ),
        out_specs=(P("pipe", "dp", None), P("pipe", "dp", None), P("pipe", "dp", None)),
        check_vma=False,
    )
```

time: 869 us -> 653 us (0.75)
  waiting for transfers between devices: 713 us -> 521 us
  Pallas kernels: 0 us -> 85.7 us
  matrix products: 70 us -> 21.2 us
  local copies, waits for them, and re-layouts: 35.1 us -> 2.64 us
  other arithmetic: 29.1 us -> 7.2 us
    ppermute x5 -> x0, waiting for transfers between devices: 172 us -> none  [passed_along(): return lax.ppermute(shard, axis, pairs)]
    pallas_call x0 -> x2, Pallas kernels: none -> 85.7 us  [the longest x1 78 us: chain(): pl.pallas_call(functools.partial(chain_kernel, micro, length, lax.axis_si...]
    dot_general x18 -> x1, matrix products: 58.5 us -> 10.2 us  [body(): preact = jnp.dot(normed, w_first, preferred_element_type=jnp.float32)]
    all_gather x1, waiting for transfers between devices: 76.9 us -> 53.5 us  [body(): w_second = lax.all_gather(w_mine, 'dp', axis=0, tiled=True)]
    reshape x8 -> x0, local copies, waits for them, and re-layouts: 10 us -> none  [the longest x2 3.57 us: attend(): active32[:, 2 * value_cols:2 * value_cols + query_cols]]
    dynamic_update_slice x4 -> x0, other arithmetic: 9.27 us -> none  [the longest x2 6.46 us: work(): lax.dynamic_update_slice_in_dim(store_now, grad_preact, start, 0)]
  transfers between devices with their start and end apart: 9 -> 4, of which waited for: 9 -> 4; matrix products, arithmetic and copies ran while one was open for 1% -> 3% of each run, Pallas kernels for 0% -> 1%
where the time goes in v1:
time: 653 us; the launch traced here: 652 us
  waiting for transfers between devices  521 us (80%)
  Pallas kernels  85.7 us (13%)
  matrix products  21.2 us (3%)
  between operations  13.8 us (2%)
  other arithmetic  7.2 us (1%)
    reduce_scatter x1, waiting for transfers between devices, body(): lax.psum_scatter(part_in, 'dp', scatter_dimension=0, tiled=True)  208 us
    all_gather x1, waiting for transfers between devices, body(): w_first = lax.all_gather(w_in[0], 'dp', axis=0, tiled=True)  181 us
    pallas_call x1, Pallas kernels, chain(): pl.pallas_call(functools.partial(chain_kernel, micro, length, lax.axis_si...  78 us
    reduce_scatter x1, waiting for transfers between devices, body(): lax.psum_scatter(part_out, 'dp', scatter_dimension=0, tiled=True)  77.8 us
    all_gather x1, waiting for transfers between devices, body(): w_second = lax.all_gather(w_mine, 'dp', axis=0, tiled=True)  53.5 us
  transfers between devices with their start and end apart: 4, of which 4 were waited for; matrix products, arithmetic and copies ran while one was open for 3% of the time, Pallas kernels for 1%

profile of v1, /device:TPU:0, one launch (start us, length us, event | category | flops | bytes accessed | tf_op | source)
XLA Modules:
  0.0 652.2 jit_solution(1695343078410556450)
XLA Ops:
  7.2 0.0 copy-start.5
  7.2 0.0 copy-start
  7.2 0.0 all-gather.6.cloned.1.call-start
  7.2 0.7 all-gather.6.cloned.1.call-update
  7.9 0.0 all-gather.4.cloned.1.call-start
  8.0 181.1 %all-gather.6.cloned.1.call-done = bf16[1,2048,3072]{2,1,0:T(8,128)(2,1)} async-done(((bf16[1,256,3072]{2,1,0:T(8,128)(2,1)}), bf16[1,2048,3072]{2,1,0:T(8,128)(2,1)}) %all-gather.6.cloned.1.call-update) | async-done | bytes 12582928 | tf_op jit(solution)/shard_map/all_gather | solution.py:285
  189.0 0.0 all-gather.4.cloned.1.call-update
  189.1 0.0 reduce-scatter.5.cloned.1.call-start
  189.1 0.0 copy-done.5
  189.1 0.2 convert_reduce_fusion.1
  189.3 0.8 convert_divide_fusion.mask_ref
  190.1 0.0 copy-done
  190.1 0.2 convert_reduce_fusion
  190.4 0.4 fusion.2
  190.8 10.2 %multiply_convert_fusion = (bf16[256,3072]{1,0:T(8,128)(2,1)}, f32[256,3072]{1,0:T(8,128)}) fusion(bf16[2048,3072]{1,0:T(8,128)(2,1)} %bitcast.32, f32[256]{0:T(256)S(1)} %add_rsqrt_fusion, f32[256]{0:T(256)S(1)} %broadcast_multiply_fusion, bf16[1,256,2048]{2,1,0:T(8,128)(2,1)S(1)} %copy-done), kind=kOutput, calls=%fused_computation.2 | convolution fusion | flops 3227254784 | bytes 18352128 | tf_op jit(solution)/shard_map/dot_general | solution.py:290
  201.0 7.7 %attend.1 = (f32[4096,128]{1,0:T(8,128)}, f32[256,1024]{1,0:T(8,128)}, f32[256,128]{1,0:T(8,128)}, bf16[256,1024]{1,0:T(8,128)(2,1)}) custom-call(bf16[256,3072]{1,0:T(8,128)(2,1)} %get-tuple-element.21.act_ref, f32[256,128]{1,0:T(8,128)} %convert_divide_fusion.mask_ref), custom_call_target="tpu_custom_call" | custom-call | tf_op jit(solution)/shard_map/attend/pallas_call | solution.py:105
  208.7 53.5 %all-gather.4.cloned.1.call-done.second_ref = bf16[1024,2048]{1,0:T(8,128)(2,1)} async-done(((bf16[128,2048]{1,0:T(8,128)(2,1)}), bf16[1024,2048]{1,0:T(8,128)(2,1)}) %all-gather.4.cloned.1.call-update) | async-done | bytes 4194320 | tf_op jit(solution)/shard_map/all_gather | solution.py:287
  262.2 78.0 %chain.1 = (bf16[256,2048]{1,0:T(8,128)(2,1)}, bf16[256,3072]{1,0:T(8,128)(2,1)}, bf16[256,2048]{1,0:T(8,128)(2,1)}) custom-call(bf16[256,2048]{1,0:T(8,128)(2,1)} %top_ref.1, bf16[256,2048]{1,0:T(8,128)(2,1)} %bitcast.31, bf16[256,3072]{1,0:T(8,128)(2,1)} %get-tuple-element.21.act_ref, f32[256,3072]{1,0:T(8,128)} %get-tuple-element.22.pre_ref, ...), custom_call_target="tpu_custom_call" | custom-call | tf_op jit(solution)/shard_map/chain/pallas_call | solution.py:247
  340.2 0.0 copy-done.3
  340.2 4.5 convolution_convert_fusion.1
  344.7 0.0 reduce-scatter.5.cloned.1.call-update
  344.7 0.0 reduce-scatter.3.cloned.1.call-start
  344.8 1.1 copy-done.1
  345.9 0.5 copy-done.2
  346.4 6.6 %convolution_convert_fusion = bf16[2048,3072]{1,0:T(8,128)(2,1)} fusion(bf16[256,3072]{1,0:T(8,128)(2,1)S(1)} %copy-done.2, f32[256]{0:T(256)S(1)} %add_rsqrt_fusion, f32[256]{0:T(256)S(1)} %broadcast_multiply_fusion, bf16[1,256,2048]{2,1,0:T(8,128)(2,1)S(1)} %copy-done.1), kind=kOutput, calls=%fused_computation | convolution fusion | flops 3229614080 | bytes 15206400 | tf_op jit(solution)/shard_map/dot_general | solution.py:51
  353.0 0.0 reduce-scatter.3.cloned.1.call-update
  353.0 77.8 %reduce-scatter.5.cloned.1.call-done = bf16[128,2048]{1,0:T(8,128)(2,1)} async-done(((bf16[1024,2048]{1,0:T(8,128)(2,1)}), bf16[128,2048]{1,0:T(8,128)(2,1)}) %reduce-scatter.5.cloned.1.call-update) | async-done | bytes 524304 | tf_op jit(solution)/shard_map/reduce_scatter | solution.py:297
  430.8 2.1 bitcast_convert_fusion.1
  432.9 208.4 %reduce-scatter.3.cloned.1.call-done = bf16[256,3072]{1,0:T(8,128)(2,1)} async-done(((bf16[2048,3072]{1,0:T(8,128)(2,1)}), bf16[256,3072]{1,0:T(8,128)(2,1)}) %reduce-scatter.3.cloned.1.call-update) | async-done | bytes 1572880 | tf_op jit(solution)/shard_map/reduce_scatter | solution.py:299
  641.3 3.4 bitcast_convert_fusion
  644.7 0.0 copy-done.4
  644.7 1.0 copy.9
  (7 shorter events, 0.0 us)
Async XLA Ops:
  7.2 182.0 %copy-start.5 = (s32[2,128]{1,0:T(2,128)S(1)}, s32[2,128]{1,0:T(2,128)}, u32[]{:S(2)}) copy-start(s32[2,128]{1,0:T(2,128)} %param.9) | copy-start | bytes 3076
  7.2 183.0 %copy-start = (bf16[1,256,2048]{2,1,0:T(8,128)(2,1)S(1)}, bf16[1,256,2048]{2,1,0:T(8,128)(2,1)}, u32[]{:S(2)}) copy-start(bf16[1,256,2048]{2,1,0:T(8,128)(2,1)} %param.5) | copy-start | bytes 3145732
  7.2 181.9 %all-gather.6.cloned.1.call-start = ((), (), s32[]{:S(2)}) async-start(), calls=%async_computation.5 | async-start | bytes 14155776 | tf_op jit(solution)/shard_map/all_gather | solution.py:285
  7.9 254.2 %all-gather.4.cloned.1.call-start = ((), (), s32[]{:S(2)}) async-start(), calls=%async_computation.2 | async-start | bytes 4718592 | tf_op jit(solution)/shard_map/all_gather | solution.py:287
  189.1 241.7 %reduce-scatter.5.cloned.1.call-start = ((), (), s32[]{:S(2)}) async-start(), calls=%async_computation.4 | async-start | bytes 4718592 | tf_op jit(solution)/shard_map/reduce_scatter | solution.py:297
  262.2 78.0 %copy-start.3 = (bf16[256,1024]{1,0:T(8,128)(2,1)S(1)}, bf16[256,1024]{1,0:T(8,128)(2,1)}, u32[]{:S(2)}) copy-start(bf16[256,1024]{1,0:T(8,128)(2,1)} %get-tuple-element.19) | copy-start | bytes 1572868
  344.7 1.2 copy-start.1
  344.7 1.7 copy-start.2
  344.7 296.6 %reduce-scatter.3.cloned.1.call-start = ((), (), s32[]{:S(2)}) async-start(), calls=%async_computation.3 | async-start | bytes 14155776 | tf_op jit(solution)/shard_map/reduce_scatter | solution.py:299
  432.9 211.8 %copy-start.4 = (bf16[256,2048]{1,0:T(8,128)(2,1)S(1)}, bf16[256,2048]{1,0:T(8,128)(2,1)}, u32[]{:S(2)}) copy-start(bf16[256,2048]{1,0:T(8,128)(2,1)} %get-tuple-element.17) | copy-start | bytes 3145732
Sparse Core Ops, SparseCore 0:
  10.2 178.8 all-gather.5
  191.2 70.9 all-gather.3
  344.8 85.9 reduce-scatter.4
  434.2 207.0 reduce-scatter.2

commit v2 on v1

--- a/solution.py
+++ b/solution.py
@@ -269,6 +269,164 @@
     )(top, inputs, activated, preact, scores, unit, rstd, mask, w_first, w_second)
 
 
+def add_into(target, left, right):
+    step = 32
+
+    def one(index, _):
+        rows = pl.ds(pl.multiple_of(index * step, step), step)
+        total = left[rows, :].astype(jnp.float32) + right[rows, :].astype(jnp.float32)
+        target[rows, :] = total.astype(target.dtype)
+        return 0
+
+    lax.fori_loop(0, target.shape[0] // step, one, 0)
+
+
+def scatter_kernel(line, part_a, part_b, out_a, out_b, *scratch):
+    pairs = (
+        (part_a, out_a) + scratch[0:4],
+        (part_b, out_b) + scratch[4:8],
+    )
+    load_sem, pair_send, pair_recv, right_send, right_recv, left_send, left_recv = scratch[8:]
+    rank = lax.axis_index("dp")
+    spot, lane_of = rank // 2, rank % 2
+    has_left, has_right = spot > 0, spot < line - 1
+    partner = spot * 2 + 1 - lane_of
+    right = jnp.minimum(spot + 1, line - 1) * 2 + lane_of
+    left = jnp.maximum(spot - 1, 0) * 2 + lane_of
+
+    barrier = pltpu.get_barrier_semaphore()
+    pl.semaphore_signal(barrier, inc=1, device_id={"dp": partner}, device_id_type=MESH)
+
+    @pl.when(has_left)
+    def _():
+        pl.semaphore_signal(barrier, inc=1, device_id={"dp": left}, device_id_type=MESH)
+
+    @pl.when(has_right)
+    def _():
+        pl.semaphore_signal(barrier, inc=1, device_id={"dp": right}, device_id_type=MESH)
+
+    pl.semaphore_wait(barrier, 1 + jnp.minimum(spot, 1) + jnp.minimum(line - 1 - spot, 1))
+
+    def block_at(turn):
+        near = jnp.minimum(spot, line - 1 - spot)
+        ahead = line - 1 - 2 * near
+        lone = jnp.where(spot <= line - 1 - spot, line - 1 - turn, turn)
+        after = jnp.maximum(turn - ahead, 0)
+        reach = near - after // 2
+        both = jnp.where(after % 2 == 0, spot + reach, spot - reach)
+        return jnp.where(turn < ahead, lone, both)
+
+    def load_of(which, block):
+        part, _, own, _, _, _ = pairs[which]
+        return pltpu.make_async_copy(part.at[block, lane_of], own.at[block], load_sem.at[which, block])
+
+    def pair_of(which, block):
+        part, _, _, paired, _, _ = pairs[which]
+        return pltpu.make_async_remote_copy(
+            src_ref=part.at[block, 1 - lane_of], dst_ref=paired.at[block],
+            send_sem=pair_send.at[which, block], recv_sem=pair_recv.at[which, block],
+            device_id={"dp": partner}, device_id_type=MESH,
+        )
+
+    def flow_of(which, block, rightward, source):
+        flow = pairs[which][4 if rightward else 5]
+        sends, recvs = (right_send, right_recv) if rightward else (left_send, left_recv)
+        return pltpu.make_async_remote_copy(
+            src_ref=source.at[block], dst_ref=flow.at[block],
+            send_sem=sends.at[which, block], recv_sem=recvs.at[which, block],
+            device_id={"dp": right if rightward else left}, device_id_type=MESH,
+        )
+
+    def begin(turn, _):
+        block = block_at(turn)
+        for which in range(2):
+            pair_of(which, block).start()
+            load_of(which, block).start()
+        return 0
+
+    lax.fori_loop(0, line, begin, 0)
+
+    def pass_on(turn, _):
+        block = block_at(turn)
+        for which in range(2):
+            own, paired = pairs[which][2:4]
+            load_of(which, block).wait()
+            pair_of(which, block).wait_recv()
+            add_into(own.at[block], own.at[block], paired.at[block])
+            for rightward in (True, False):
+                flow = pairs[which][4 if rightward else 5]
+                fed = has_left if rightward else has_right
+                wanted = block > spot if rightward else block < spot
+
+                @pl.when(jnp.logical_and(wanted, fed))
+                def _():
+                    flow_of(which, block, rightward, flow).wait_recv()
+                    add_into(flow.at[block], flow.at[block], own.at[block])
+                    flow_of(which, block, rightward, flow).start()
+
+                @pl.when(jnp.logical_and(wanted, jnp.logical_not(fed)))
+                def _():
+                    flow_of(which, block, rightward, own).start()
+        return 0
+
+    lax.fori_loop(0, line, pass_on, 0)
+
+    for which in range(2):
+        out, own = pairs[which][1:3]
+        for rightward in (True, False):
+            flow = pairs[which][4 if rightward else 5]
+
+            @pl.when(has_left if rightward else has_right)
+            def _():
+                flow_of(which, spot, rightward, flow).wait_recv()
+
+        @pl.when(jnp.logical_and(has_left, has_right))
+        def _():
+            add_into(out, own.at[spot], pairs[which][4].at[spot])
+            add_into(out, out, pairs[which][5].at[spot])
+
+        @pl.when(jnp.logical_and(has_left, jnp.logical_not(has_right)))
+        def _():
+            add_into(out, own.at[spot], pairs[which][4].at[spot])
+
+        @pl.when(jnp.logical_and(has_right, jnp.logical_not(has_left)))
+        def _():
+            add_into(out, own.at[spot], pairs[which][5].at[spot])
+
+    def finish(block, _):
+        for which in range(2):
+            pair_of(which, block).wait_send()
+            for rightward in (True, False):
+
+                @pl.when(block > spot if rightward else block < spot)
+                def _():
+                    flow_of(which, block, rightward, pairs[which][2]).wait_send()
+        return 0
+
+    lax.fori_loop(0, line, finish, 0)
+
+
+def scatter_sums(part_a, part_b):
+    devices = lax.axis_size("dp")
+    line = devices // 2
+    parts = [part.reshape(line, 2, part.shape[0] // devices, part.shape[1]) for part in (part_a, part_b)]
+    scratch = []
+    for part in parts:
+        scratch += [pltpu.VMEM((line,) + part.shape[2:], part.dtype)] * 4
+    scratch += [pltpu.SemaphoreType.DMA((2, line))] * 7
+    return pl.pallas_call(
+        functools.partial(scatter_kernel, line),
+        out_shape=tuple(jax.ShapeDtypeStruct(part.shape[2:], jnp.float32) for part in parts),
+        in_specs=[pl.BlockSpec(memory_space=pl.ANY)] * 2,
+        out_specs=(VMEM,) * 2,
+        scratch_shapes=scratch,
+        compiler_params=pltpu.CompilerParams(
+            collective_id=1, has_side_effects=True, vmem_limit_bytes=60 * 1024 * 1024
+        ),
+        name="scatter_sums",
+    )(*parts)
+
+
 def mask_of(segments):
     length = segments.shape[1]
     same = segments[:, :, None] == segments[:, None, :]
@@ -294,9 +452,8 @@
         top_grad, inputs, activated, preact, scores, unit, rstd, mask, w_first, w_second, micro, length
     )
     part_out = contract_rows(gated, upstream).astype(jnp.bfloat16)
-    grad_out = lax.psum_scatter(part_out, "dp", scatter_dimension=0, tiled=True).astype(jnp.float32)
     part_in = contract_rows(normed, grad_preact).astype(jnp.bfloat16)
-    grad_first = lax.psum_scatter(part_in, "dp", scatter_dimension=0, tiled=True).astype(jnp.float32)
+    grad_first, grad_out = scatter_sums(part_in, part_out)
     return (grads[None], grad_first[None], grad_out[None])
 
 

time: 653 us -> 539 us (0.83)
  waiting for transfers between devices: 521 us -> 235 us
  Pallas kernels: 85.7 us -> 261 us
    reduce_scatter x2 -> x0, waiting for transfers between devices: 286 us -> none  [the longest x1 208 us: body(): lax.psum_scatter(part_in, 'dp', scatter_dimension=0, tiled=True)]
    pallas_call x0 -> x1, Pallas kernels: none -> 175 us  [scatter_sums(): pl.pallas_call(functools.partial(scatter_kernel, line), out_shape=tuple((...]
  transfers between devices with their start and end apart: 4 -> 2, of which waited for: 4 -> 2; matrix products, arithmetic and copies ran while one was open for 3% -> 2% of each run, Pallas kernels for 1% -> 1%
where the time goes in v2:
time: 539 us
  Pallas kernels  261 us (48%)
  waiting for transfers between devices  235 us (44%)
  matrix products  21.5 us (4%)
  between operations  14.1 us (3%)
  local copies, waits for them, and re-layouts  5.96 us (1%)
    all_gather x1, waiting for transfers between devices, body(): w_first = lax.all_gather(w_in[0], 'dp', axis=0, tiled=True)  181 us
    pallas_call x1, Pallas kernels, scatter_sums(): pl.pallas_call(functools.partial(scatter_kernel, line), out_shape=tuple((...  175 us
    pallas_call x1, Pallas kernels, chain(): pl.pallas_call(functools.partial(chain_kernel, micro, length, lax.axis_si...  78 us
    all_gather x1, waiting for transfers between devices, body(): w_second = lax.all_gather(w_mine, 'dp', axis=0, tiled=True)  53.5 us
    dot_general x2, matrix products, contract_rows(): lax.dot_general(left, right, (((0,), (0,)), ((), ())), preferred_element_...  11.3 us
  transfers between devices with their start and end apart: 2, of which 2 were waited for; matrix products, arithmetic and copies ran while one was open for 2% of the time, Pallas kernels for 1%

profile of v2, /device:TPU:0, one launch (start us, length us, event | category | flops | bytes accessed | tf_op | source)
XLA Modules:
  0.0 539.2 jit_solution(2776009500681768297)
XLA Ops:
  7.2 0.0 copy-start.6
  7.2 0.0 copy-start
  7.2 0.0 all-gather.6.cloned.1.call-start
  7.2 0.7 all-gather.6.cloned.1.call-update
  7.9 0.0 all-gather.4.cloned.1.call-start
  8.0 181.1 %all-gather.6.cloned.1.call-done = bf16[1,2048,3072]{2,1,0:T(8,128)(2,1)} async-done(((bf16[1,256,3072]{2,1,0:T(8,128)(2,1)}), bf16[1,2048,3072]{2,1,0:T(8,128)(2,1)}) %all-gather.6.cloned.1.call-update) | async-done | bytes 12582928 | tf_op jit(solution)/shard_map/all_gather | solution.py:443
  189.0 0.0 all-gather.4.cloned.1.call-update
  189.1 0.0 copy-done.6
  189.1 0.2 convert_reduce_fusion.1
  189.3 0.8 convert_divide_fusion.mask_ref
  190.1 0.0 copy-done
  190.1 0.2 convert_reduce_fusion
  190.3 0.4 fusion.2
  190.7 10.2 %multiply_convert_fusion = (bf16[256,3072]{1,0:T(8,128)(2,1)}, f32[256,3072]{1,0:T(8,128)}) fusion(bf16[2048,3072]{1,0:T(8,128)(2,1)} %bitcast.32, f32[256]{0:T(256)S(1)} %add_rsqrt_fusion, f32[256]{0:T(256)S(1)} %broadcast_multiply_fusion, bf16[1,256,2048]{2,1,0:T(8,128)(2,1)S(1)} %copy-done), kind=kOutput, calls=%fused_computation.2 | convolution fusion | flops 3227254784 | bytes 18352128 | tf_op jit(solution)/shard_map/dot_general | solution.py:448
  201.0 7.7 %attend.1 = (f32[4096,128]{1,0:T(8,128)}, f32[256,1024]{1,0:T(8,128)}, f32[256,128]{1,0:T(8,128)}, bf16[256,1024]{1,0:T(8,128)(2,1)}) custom-call(bf16[256,3072]{1,0:T(8,128)(2,1)} %get-tuple-element.25.act_ref, f32[256,128]{1,0:T(8,128)} %convert_divide_fusion.mask_ref), custom_call_target="tpu_custom_call" | custom-call | tf_op jit(solution)/shard_map/attend/pallas_call | solution.py:105
  208.6 53.5 %all-gather.4.cloned.1.call-done.second_ref = bf16[1024,2048]{1,0:T(8,128)(2,1)} async-done(((bf16[128,2048]{1,0:T(8,128)(2,1)}), bf16[1024,2048]{1,0:T(8,128)(2,1)}) %all-gather.4.cloned.1.call-update) | async-done | bytes 4194320 | tf_op jit(solution)/shard_map/all_gather | solution.py:445
  262.2 0.0 copy-start.1
  262.2 78.0 %chain.1 = (bf16[256,2048]{1,0:T(8,128)(2,1)}, bf16[256,3072]{1,0:T(8,128)(2,1)}, bf16[256,2048]{1,0:T(8,128)(2,1)}) custom-call(bf16[256,2048]{1,0:T(8,128)(2,1)} %top_ref.1, bf16[256,2048]{1,0:T(8,128)(2,1)} %bitcast.31, bf16[256,3072]{1,0:T(8,128)(2,1)} %get-tuple-element.25.act_ref, f32[256,3072]{1,0:T(8,128)} %get-tuple-element.26.pre_ref, ...), custom_call_target="tpu_custom_call" | custom-call | tf_op jit(solution)/shard_map/chain/pallas_call | solution.py:247
  340.2 0.0 copy-done.1
  340.2 0.0 copy-start.2
  340.2 0.0 copy-start.5
  340.3 8.1 %convolution_convert_fusion = bf16[2048,3072]{1,0:T(8,128)(2,1)} fusion(bf16[256,3072]{1,0:T(8,128)(2,1)} %get-tuple-element.20, f32[256]{0:T(256)S(1)} %add_rsqrt_fusion, f32[256]{0:T(256)S(1)} %broadcast_multiply_fusion, bf16[1,256,2048]{2,1,0:T(8,128)(2,1)S(1)} %copy-done.1), kind=kOutput, calls=%fused_computation | convolution fusion | flops 3229614080 | bytes 15206400 | tf_op jit(solution)/shard_map/dot_general | solution.py:51
  348.3 0.0 copy-done.2
  348.4 0.0 copy-done.5
  348.4 3.2 convolution_convert_fusion.1
  351.6 0.0 copy-start.3
  351.6 174.8 %scatter_sums.1 = (f32[256,3072]{1,0:T(8,128)}, f32[128,2048]{1,0:T(8,128)}) custom-call(bf16[4,2,256,3072]{3,2,1,0:T(8,128)(2,1)} %bitcast.29, bf16[4,2,128,2048]{3,2,1,0:T(8,128)(2,1)} %bitcast.30), custom_call_target="tpu_custom_call" | custom-call | tf_op jit(solution)/shard_map/scatter_sums/pallas_call | solution.py:417
  526.4 0.0 copy-done.3
  526.4 1.0 copy.11
  527.4 4.0 copy.12
  531.3 0.0 copy-done.4
  531.3 1.0 copy.13
  (4 shorter events, 0.0 us)
Async XLA Ops:
  7.2 181.9 %copy-start.6 = (s32[2,128]{1,0:T(2,128)S(1)}, s32[2,128]{1,0:T(2,128)}, u32[]{:S(2)}) copy-start(s32[2,128]{1,0:T(2,128)} %param.9) | copy-start | bytes 3076
  7.2 182.9 %copy-start = (bf16[1,256,2048]{2,1,0:T(8,128)(2,1)S(1)}, bf16[1,256,2048]{2,1,0:T(8,128)(2,1)}, u32[]{:S(2)}) copy-start(bf16[1,256,2048]{2,1,0:T(8,128)(2,1)} %param.5) | copy-start | bytes 3145732
  7.2 181.9 %all-gather.6.cloned.1.call-start = ((), (), s32[]{:S(2)}) async-start(), calls=%async_computation.1 | async-start | bytes 14155776 | tf_op jit(solution)/shard_map/all_gather | solution.py:443
  7.9 254.2 %all-gather.4.cloned.1.call-start = ((), (), s32[]{:S(2)}) async-start(), calls=%async_computation | async-start | bytes 4718592 | tf_op jit(solution)/shard_map/all_gather | solution.py:445
  262.2 78.1 %copy-start.1 = (bf16[1,256,2048]{2,1,0:T(8,128)(2,1)S(1)}, bf16[1,256,2048]{2,1,0:T(8,128)(2,1)}, u32[]{:S(2)}) copy-start(bf16[1,256,2048]{2,1,0:T(8,128)(2,1)} %param.5) | copy-start | bytes 3145732
  340.2 8.1 %copy-start.2 = (bf16[256,1024]{1,0:T(8,128)(2,1)S(1)}, bf16[256,1024]{1,0:T(8,128)(2,1)}, u32[]{:S(2)}) copy-start(bf16[256,1024]{1,0:T(8,128)(2,1)} %get-tuple-element.21) | copy-start | bytes 1572868
  340.2 8.1 %copy-start.5 = (bf16[256,2048]{1,0:T(8,128)(2,1)S(1)}, bf16[256,2048]{1,0:T(8,128)(2,1)}, u32[]{:S(2)}) copy-start(bf16[256,2048]{1,0:T(8,128)(2,1)} %get-tuple-element.22) | copy-start | bytes 3145732
  351.6 174.8 %copy-start.3 = (bf16[256,2048]{1,0:T(8,128)(2,1)S(1)}, bf16[256,2048]{1,0:T(8,128)(2,1)}, u32[]{:S(2)}) copy-start(bf16[256,2048]{1,0:T(8,128)(2,1)} %get-tuple-element.19) | copy-start | bytes 3145732
  527.4 4.0 copy-start.4
Sparse Core Ops, SparseCore 0:
  10.2 178.8 all-gather.5
  191.2 70.9 all-gather.3
